TPU v7x, 32 devices: a whole 2x2x4 slice. The times are simulated.
32 devices in a mesh: dp: 8 (over y, x, core), seq: 4 (over z).
Axes of the slice: x: 2, y: 2, z: 4, core: 2. Of those that a mesh axis runs over, the one named last changes fastest.
Arguments:
- hidden_in: bfloat16 [24, 2048, 1024], P('dp', 'seq'), may hold values from -6 to 6
- cotangent: bfloat16 [24, 2048, 1024], P('dp', 'seq'), may hold values from -6 to 6
- first_gain: bfloat16 [1024], P(('dp', 'seq')), may hold values from 0.099609375 to 1.8984375
- first_shift: bfloat16 [1024], P(('dp', 'seq')), may hold values from -3 to 3
- triple_weight: bfloat16 [1024, 3072], P(('dp', 'seq')), may hold values from -0.1875 to 0.1875
- triple_bias: bfloat16 [3072], P(('dp', 'seq')), may hold values from -3 to 3
- dense_weight: bfloat16 [1024, 1024], P(('dp', 'seq')), may hold values from -0.75 to 0.75
- dense_bias: bfloat16 [1024], P(('dp', 'seq')), may hold values from -3 to 3
- second_gain: bfloat16 [1024], P(('dp', 'seq')), may hold values from 0.099609375 to 1.8984375
- second_shift: bfloat16 [1024], P(('dp', 'seq')), may hold values from -3 to 3
- expand_weight: bfloat16 [1024, 4096], P(('dp', 'seq')), may hold values from -0.1875 to 0.1875
- expand_bias: bfloat16 [4096], P(('dp', 'seq')), may hold values from -3 to 3
- contract_weight: bfloat16 [4096, 1024], P(('dp', 'seq')), may hold values from -0.09375 to 0.09375
- contract_bias: bfloat16 [1024], P(('dp', 'seq')), may hold values from -3 to 3
Outputs:
- block_out: bfloat16 [24, 2048, 1024], P('dp', 'seq')
- grad_input: float32 [24, 2048, 1024], P('dp', 'seq')
- grad_first_gain: float32 [1024], P(('dp', 'seq'))
- grad_first_shift: float32 [1024], P(('dp', 'seq'))
- grad_triple_weight: float32 [1024, 3072], P(('dp', 'seq'))
- grad_triple_bias: float32 [3072], P(('dp', 'seq'))
- grad_dense_weight: float32 [1024, 1024], P(('dp', 'seq'))
- grad_dense_bias: float32 [1024], P(('dp', 'seq'))
- grad_second_gain: float32 [1024], P(('dp', 'seq'))
- grad_second_shift: float32 [1024], P(('dp', 'seq'))
- grad_expand_weight: float32 [1024, 4096], P(('dp', 'seq'))
- grad_expand_bias: float32 [4096], P(('dp', 'seq'))
- grad_contract_weight: float32 [4096, 1024], P(('dp', 'seq'))
- grad_contract_bias: float32 [1024], P(('dp', 'seq'))
All inputs are finite; a program needn't handle non-finite values.
Results may differ from a plain program's by a relative error of at most 0.0098.
Values may be sent and summed in bfloat16 or wider, within the bound.
A program may use at most 448 MiB of HBM per device.

v0:
```python
import math

import jax
import jax.numpy as jnp
from jax import lax
from jax.sharding import PartitionSpec as P

H = 16
HD = 64
ROT = 16


big_negative = -1e30
epsilon = 1e-05


def layer_norm(values, gain, shift):
    average = jnp.mean(values, axis=-1, keepdims=True)
    centered = values - average
    variance = jnp.mean(centered * centered, axis=-1, keepdims=True)
    return centered * lax.rsqrt(variance + epsilon) * gain + shift


def rotary_tables(positions, rotary):
    half = rotary // 2
    frequency = 10000.0 ** (-(jnp.arange(half, dtype=jnp.float32) * 2.0 / rotary))
    angles = positions.astype(jnp.float32)[:, None] * frequency[None, :]
    angles = jnp.concatenate([angles, angles], axis=-1)
    return (jnp.cos(angles), jnp.sin(angles))


def rotate(values, cosine, sine):
    rotary = cosine.shape[-1]
    half = rotary // 2
    leading = values[..., :rotary]
    turned = jnp.concatenate([-leading[..., half:], leading[..., :half]], axis=-1)
    return jnp.concatenate([leading * cosine + turned * sine, values[..., rotary:]], axis=-1)


def masked_scores(query_block, keys, start, scale):
    scores = (
        jnp.einsum("sbhe,slhe->shbl", query_block, keys, preferred_element_type=jnp.float32) * scale
    )
    shape = (query_block.shape[1], keys.shape[1])
    rows = start + lax.broadcasted_iota(jnp.int32, shape, 0)
    columns = lax.broadcasted_iota(jnp.int32, shape, 1)
    return jnp.where(columns <= rows, scores, big_negative)


def attend_forward(query, keys, values, block, scale):
    count = query.shape[1] // block

    def one_block(index):
        start = index * block
        query_block = lax.dynamic_slice_in_dim(query, start, block, 1)
        masked = masked_scores(query_block, keys, start, scale)
        highest = jnp.max(masked, axis=-1, keepdims=True)
        weights = jnp.exp(masked - highest)
        total = jnp.sum(weights, axis=-1, keepdims=True)
        probability = (weights / total).astype(jnp.bfloat16)
        context = jnp.einsum(
            "shbl,slhe->sbhe", probability, values, preferred_element_type=jnp.float32
        )
        return (context.astype(jnp.bfloat16), (highest + jnp.log(total))[..., 0])

    return lax.map(one_block, jnp.arange(count, dtype=jnp.int32))


def attend_backward(query, keys, values, grad_context, log_totals, block, scale):
    count = query.shape[1] // block

    def one_block(carry, pieces):
        grad_keys, grad_values = carry
        index, log_total = pieces
        start = index * block
        query_block = lax.dynamic_slice_in_dim(query, start, block, 1)
        grad_block = lax.dynamic_slice_in_dim(grad_context, start, block, 1)
        masked = masked_scores(query_block, keys, start, scale)
        probability = jnp.exp(masked - log_total[..., None])
        rounded = probability.astype(jnp.bfloat16)
        grad_values = grad_values + jnp.einsum(
            "shbl,sbhe->slhe", rounded, grad_block, preferred_element_type=jnp.float32
        )
        grad_prob = jnp.einsum(
            "sbhe,slhe->shbl", grad_block, values, preferred_element_type=jnp.float32
        )
        inner = jnp.sum(grad_prob * probability, axis=-1, keepdims=True)
        grad_scores = (probability * (grad_prob - inner)).astype(jnp.bfloat16)
        grad_query = (
            jnp.einsum("shbl,slhe->sbhe", grad_scores, keys, preferred_element_type=jnp.float32)
            * scale
        )
        grad_keys = (
            grad_keys
            + jnp.einsum(
                "shbl,sbhe->slhe", grad_scores, query_block, preferred_element_type=jnp.float32
            )
            * scale
        )
        return ((grad_keys, grad_values), grad_query.astype(jnp.bfloat16))

    zeros = jnp.zeros(keys.shape, jnp.float32)
    indices = jnp.arange(count, dtype=jnp.int32)
    (grad_keys, grad_values), grad_queries = lax.scan(
        one_block, (zeros, zeros), (indices, log_totals)
    )
    return (grad_queries, grad_keys, grad_values)


def local(
    hidden_in,
    cotangent,
    first_gain,
    first_shift,
    triple_weight,
    triple_bias,
    dense_weight,
    dense_bias,
    second_gain,
    second_shift,
    expand_weight,
    expand_bias,
    contract_weight,
    contract_bias,
):
    gathered = (
        lax.all_gather(first_gain, ("dp", "seq"), axis=0, tiled=True),
        lax.all_gather(first_shift, ("dp", "seq"), axis=0, tiled=True),
        lax.all_gather(triple_weight, ("dp", "seq"), axis=0, tiled=True),
        lax.all_gather(triple_bias, ("dp", "seq"), axis=0, tiled=True),
        lax.all_gather(dense_weight, ("dp", "seq"), axis=0, tiled=True),
        lax.all_gather(dense_bias, ("dp", "seq"), axis=0, tiled=True),
        lax.all_gather(second_gain, ("dp", "seq"), axis=0, tiled=True),
        lax.all_gather(second_shift, ("dp", "seq"), axis=0, tiled=True),
        lax.all_gather(expand_weight, ("dp", "seq"), axis=0, tiled=True),
        lax.all_gather(expand_bias, ("dp", "seq"), axis=0, tiled=True),
        lax.all_gather(contract_weight, ("dp", "seq"), axis=0, tiled=True),
        lax.all_gather(contract_bias, ("dp", "seq"), axis=0, tiled=True),
    )
    (
        gain_one,
        shift_one,
        w_triple,
        b_triple,
        w_dense,
        b_dense,
        gain_two,
        shift_two,
        w_expand,
        b_expand,
        w_contract,
        b_contract,
    ) = gathered
    seqs, part_len, width = hidden_in.shape
    groups = lax.axis_size("seq")
    heads_here = H // groups
    tokens_here = seqs * part_len
    scale = 1.0 / math.sqrt(HD)
    source = hidden_in.astype(jnp.float32).reshape(tokens_here, width)
    normed_one, pull_one = jax.vjp(
        layer_norm, source, gain_one.astype(jnp.float32), shift_one.astype(jnp.float32)
    )
    normed_two, pull_two = jax.vjp(
        layer_norm, source, gain_two.astype(jnp.float32), shift_two.astype(jnp.float32)
    )
    low_one = normed_one.astype(jnp.bfloat16)
    low_two = normed_two.astype(jnp.bfloat16)
    triple = jnp.dot(low_one, w_triple, preferred_element_type=jnp.float32) + b_triple.astype(
        jnp.float32
    )
    triple = triple.reshape(tokens_here, 3, H, HD)
    positions = lax.axis_index("seq") * part_len + jnp.arange(part_len, dtype=jnp.int32)
    cosine, sine = rotary_tables(jnp.tile(positions, seqs), ROT)
    cosine = cosine[:, None, :]
    sine = sine[:, None, :]

    def rotate_pair(query_part, keys_part):
        return (rotate(query_part, cosine, sine), rotate(keys_part, cosine, sine))

    (query_turned, keys_turned), pull_turn = jax.vjp(rotate_pair, triple[:, 0], triple[:, 1])
    sending = jnp.stack([query_turned, keys_turned, triple[:, 2]], axis=1).astype(jnp.bfloat16)
    sending = sending.reshape(seqs, part_len, 3, width)
    received = lax.all_to_all(sending, "seq", split_axis=3, concat_axis=1, tiled=True)
    length = received.shape[1]
    block = 512
    query = received[:, :, 0].reshape(seqs, length, heads_here, HD)
    keys = received[:, :, 1].reshape(seqs, length, heads_here, HD)
    values = received[:, :, 2].reshape(seqs, length, heads_here, HD)
    contexts, log_totals = attend_forward(query, keys, values, block, scale)
    context_heads = contexts.transpose(1, 0, 2, 3, 4).reshape(seqs, length, heads_here * HD)
    context_tokens = lax.all_to_all(context_heads, "seq", split_axis=1, concat_axis=2, tiled=True)
    context_flat = context_tokens.reshape(tokens_here, width)
    attended = jnp.dot(context_flat, w_dense, preferred_element_type=jnp.float32) + b_dense.astype(
        jnp.float32
    )
    expanded = jnp.dot(low_two, w_expand, preferred_element_type=jnp.float32) + b_expand.astype(
        jnp.float32
    )
    activated, pull_gelu = jax.vjp(lambda inner: jax.nn.gelu(inner, approximate=False), expanded)
    low_act = activated.astype(jnp.bfloat16)
    contracted = jnp.dot(
        low_act, w_contract, preferred_element_type=jnp.float32
    ) + b_contract.astype(jnp.float32)
    block_out = (source + attended + contracted).astype(jnp.bfloat16).reshape(seqs, part_len, width)
    w_triple_back, w_dense_back, w_expand_back, w_contract_back = (
        w_triple,
        w_dense,
        w_expand,
        w_contract,
    )
    upstream = cotangent.reshape(tokens_here, width)
    upstream_total = jnp.sum(upstream.astype(jnp.float32), axis=0)
    grad_context = jnp.einsum(
        "td,ed->te", upstream, w_dense_back, preferred_element_type=jnp.float32
    )
    grad_context = grad_context.astype(jnp.bfloat16).reshape(seqs, part_len, width)
    grad_context_heads = lax.all_to_all(
        grad_context, "seq", split_axis=2, concat_axis=1, tiled=True
    )
    grad_w_dense = jnp.einsum(
        "td,te->de", context_flat, upstream, preferred_element_type=jnp.float32
    )
    grad_act = jnp.einsum(
        "td,fd->tf", upstream, w_contract_back, preferred_element_type=jnp.float32
    )
    grad_expanded = pull_gelu(grad_act)[0].astype(jnp.bfloat16)
    grad_w_contract = jnp.einsum("tf,td->fd", low_act, upstream, preferred_element_type=jnp.float32)
    grad_w_expand = jnp.einsum(
        "td,tf->df", low_two, grad_expanded, preferred_element_type=jnp.float32
    )
    grad_b_expand = jnp.sum(grad_expanded.astype(jnp.float32), axis=0)
    grad_second = jnp.einsum(
        "tf,df->td", grad_expanded, w_expand_back, preferred_element_type=jnp.float32
    )
    grad_source_two, grad_gain_two, grad_shift_two = pull_two(grad_second)
    grad_queries, grad_keys, grad_values = attend_backward(
        query,
        keys,
        values,
        grad_context_heads.reshape(seqs, length, heads_here, HD),
        log_totals,
        block,
        scale,
    )
    grad_query_heads = grad_queries.transpose(1, 0, 2, 3, 4).reshape(seqs, length, heads_here * HD)
    grad_stack = jnp.stack(
        [
            grad_query_heads,
            grad_keys.astype(jnp.bfloat16).reshape(seqs, length, heads_here * HD),
            grad_values.astype(jnp.bfloat16).reshape(seqs, length, heads_here * HD),
        ],
        axis=2,
    )
    grad_tokens = lax.all_to_all(grad_stack, "seq", split_axis=1, concat_axis=3, tiled=True)
    grad_tokens = grad_tokens.reshape(tokens_here, 3, H, HD)
    grad_query_pre, grad_keys_pre = pull_turn(
        (grad_tokens[:, 0].astype(jnp.float32), grad_tokens[:, 1].astype(jnp.float32))
    )
    grad_triple = jnp.stack(
        [grad_query_pre, grad_keys_pre, grad_tokens[:, 2].astype(jnp.float32)], axis=1
    )
    grad_triple = grad_triple.astype(jnp.bfloat16).reshape(tokens_here, 3 * width)
    grad_w_triple = jnp.einsum(
        "td,te->de", low_one, grad_triple, preferred_element_type=jnp.float32
    )
    grad_b_triple = jnp.sum(grad_triple.astype(jnp.float32), axis=0)
    grad_first = jnp.einsum(
        "te,de->td", grad_triple, w_triple_back, preferred_element_type=jnp.float32
    )
    grad_source_one, grad_gain_one, grad_shift_one = pull_one(grad_first)
    grad_input = (upstream.astype(jnp.float32) + grad_source_one + grad_source_two).reshape(
        seqs, part_len, width
    )
    all_shards = (
        lax.psum_scatter(grad_gain_one, ("dp", "seq"), scatter_dimension=0, tiled=True),
        lax.psum_scatter(grad_shift_one, ("dp", "seq"), scatter_dimension=0, tiled=True),
        lax.psum_scatter(grad_w_triple, ("dp", "seq"), scatter_dimension=0, tiled=True),
        lax.psum_scatter(grad_b_triple, ("dp", "seq"), scatter_dimension=0, tiled=True),
        lax.psum_scatter(grad_w_dense, ("dp", "seq"), scatter_dimension=0, tiled=True),
        lax.psum_scatter(upstream_total, ("dp", "seq"), scatter_dimension=0, tiled=True),
        lax.psum_scatter(grad_gain_two, ("dp", "seq"), scatter_dimension=0, tiled=True),
        lax.psum_scatter(grad_shift_two, ("dp", "seq"), scatter_dimension=0, tiled=True),
        lax.psum_scatter(grad_w_expand, ("dp", "seq"), scatter_dimension=0, tiled=True),
        lax.psum_scatter(grad_b_expand, ("dp", "seq"), scatter_dimension=0, tiled=True),
        lax.psum_scatter(grad_w_contract, ("dp", "seq"), scatter_dimension=0, tiled=True),
        lax.psum_scatter(upstream_total, ("dp", "seq"), scatter_dimension=0, tiled=True),
    )
    (
        out_gain_one,
        out_shift_one,
        out_w_triple,
        out_b_triple,
        out_w_dense,
        out_b_dense,
        out_gain_two,
        out_shift_two,
        out_w_expand,
        out_b_expand,
        out_w_contract,
        out_b_contract,
    ) = all_shards
    return (
        block_out,
        grad_input,
        out_gain_one,
        out_shift_one,
        out_w_triple,
        out_b_triple,
        out_w_dense,
        out_b_dense,
        out_gain_two,
        out_shift_two,
        out_w_expand,
        out_b_expand,
        out_w_contract,
        out_b_contract,
    )


def solution(mesh):
    placed = (
        P("dp", "seq", None),
        P("dp", "seq", None),
        P(("dp", "seq")),
        P(("dp", "seq")),
        P(("dp", "seq"), None),
        P(("dp", "seq")),
        P(("dp", "seq"), None),
        P(("dp", "seq")),
        P(("dp", "seq")),
        P(("dp", "seq")),
        P(("dp", "seq"), None),
        P(("dp", "seq")),
        P(("dp", "seq"), None),
        P(("dp", "seq")),
    )
    return jax.shard_map(
        local,
        mesh=mesh,
        in_specs=placed,
        out_specs=(
            P("dp", "seq", None),
            P("dp", "seq", None),
            P(("dp", "seq")),
            P(("dp", "seq")),
            P(("dp", "seq"), None),
            P(("dp", "seq")),
            P(("dp", "seq"), None),
            P(("dp", "seq")),
            P(("dp", "seq")),
            P(("dp", "seq")),
            P(("dp", "seq"), None),
            P(("dp", "seq")),
            P(("dp", "seq"), None),
            P(("dp", "seq")),
        ),
        check_vma=False,
    )
```

profile of v0, /device:TPU:0, one launch (start us, length us, event | category | flops | bytes accessed | tf_op | source)
XLA Modules:
  0.0 2566.3 jit_solution(5503758318342624451)
XLA Ops:
  15.8 43.2 %all-reduce.23 = (bf16[1024]{0:T(1024)(128)(2,1)S(1)}, bf16[1024]{0:T(1024)(128)(2,1)S(1)}, bf16[3072]{0:T(1024)(128)(2,1)S(1)}, bf16[1024]{0:T(1024)(128)(2,1)S...) all-reduce(bf16[1024]{0:T(1024)(128)(2,1)S(1)} %dynamic-update-slic, ...), channel_id=1, replica_groups=mesh['dp'=8,'seq'=4] {'dp','seq'}, use_global_device_ids=true, to_apply=%add.9 | all-reduce | flops 9216 | bytes 36864
  64.5 18.8 all-gather.6.cloned.1.call-done
  188.2 312.6 %all-to-all-done = bf16[3,512,3,1024]{1,0,2,3:T(4,128)(2,1)} async-done(((bf16[3,512,3,1024]{1,0,2,3:T(4,128)(2,1)}), bf16[3,512,3,1024]{1,0,2,3:T(4,128)(2,1)}, u32[]{:S(2)}, u32[]{:S(2)}) %all-to-all-start) | async-done | bytes 9437216 | tf_op jit(solution)/shard_map/all_to_all | solution.py:183
  544.4 271.8 %while.27 = (s32[]{:T(128)}, bf16[4,3,512,4,64]{2,4,3,1,0:T(8,128)(2,1)}, f32[4,3,4,512]{3,2,1,0:T(4,128)}, s32[4]{0:T(128)S(1)}, bf16[3,2048,4,64]{1,3,2,0:T(8,...) while((s32[]{:T(128)}, ...), condition=%wide.region_5.6_spmd, body=%wide.region_2.5_spmd.sunk | while | flops 3373656576 | bytes 163255472 | solution.py:66
  546.3 21.9 fusion.134
  568.2 21.9 fusion.135
  590.7 21.7 fusion.136
  614.3 21.9 fusion.134
  636.2 21.9 fusion.135
  658.7 21.7 fusion.136
  682.2 21.9 fusion.134
  704.1 21.9 fusion.135
  726.6 21.7 fusion.136
  750.2 21.9 fusion.134
  772.1 21.9 fusion.135
  794.6 21.7 fusion.136
  845.5 153.6 %all-gather = bf16[32,1,128]{2,1,0:T(2,128)(2,1)S(1)} all-gather(bf16[1,1,128]{2,1,0:T(2,128)(2,1)S(1)} %bitcast.225), channel_id=1, replica_groups=mesh['dp'=8,'seq'=4] {'dp','seq'}, dimensions={0}, use_global_device_ids=true | all-gather | bytes 8448 | tf_op jit(solution)/shard_map/all_gather | solution.py:136
  1012.1 70.8 %multiply_convert_fusion.2 = (bf16[1536,4096]{1,0:T(8,128)(2,1)}, f32[1536,4096]{1,0:T(8,128)}, f32[1536,4096]{1,0:T(8,128)}) fusion(f32[4096]{0:T(1024)S(1)} %bitcast.223, bf16[1536,1024]{1,0:T(8,128)(2,1)} %get-tuple-element.239, bf16[1024,4096]{1,0:T(8,128)(2,1)} %all-gather.10.cloned.1.call-done), kind=kOutput, calls=%fused_computation.47 | convolution fusion | flops 13300137984 | bytes 74465280 | tf_op jit(solution)/shard_map/dot_general | solution.py:196
  1082.9 33.2 %convert_reduce_fusion = (f32[4096]{0:T(1024)}, bf16[1536,4096]{1,0:T(8,128)(2,1)}) fusion(f32[1536,4096]{1,0:T(8,128)} %get-tuple-element.222, bf16[1536,1024]{1,0:T(8,128)(2,1)S(1)} %bitcast.208, bf16[4096,1024]{1,0:T(8,128)(2,1)} %all-gather.12.cloned.1.call-done, f32[1536,4096]{1,0:T(8,128)} %get-tuple-element.259, f32[4096]{0:T(1024)S(1)} %bitcast.224), kind=kOutput, calls=%fused_computation.45 | convolution fusion | flops 12991852544 | bytes 74481664 | tf_op jit(solution)/shard_map/td,fd->tf/dot_general | solution.py:223
  1116.1 19.8 fusion.83
  1155.1 170.3 %all-to-all-done.2 = bf16[3,512,1024]{1,0,2:T(4,128)(2,1)} async-done(((bf16[3,512,1024]{1,0,2:T(4,128)(2,1)}), bf16[3,512,1024]{1,0,2:T(4,128)(2,1)}, u32[]{:S(2)}, u32[]{:S(2)}) %all-to-all-start.2) | async-done | bytes 3145760 | tf_op jit(solution)/shard_map/all_to_all | solution.py:217
  1338.4 19.7 fusion.84
  1360.1 638.2 %while.28 = (s32[]{:T(128)}, f32[3,2048,4,64]{1,3,2,0:T(8,128)}, f32[3,2048,4,64]{1,3,2,0:T(8,128)}, bf16[4,3,512,4,64]{2,4,3,1,0:T(8,128)(2,1)}, s32[4]{0:T(128...) while((s32[]{:T(128)}, f32[3,2048,4,64]{1,3,2,0:T(8,128)}, ...), condition=%wide.region_8.9_spmd.clone, body=%wide.region_6.0_spmd.clone.sunk | while | flops 8251501056 | bytes 420393664 | solution.py:104
  1361.8 21.6 fusion.146
  1384.8 37.7 %multiply_reduce_fusion.2 = (f32[3,4,512]{2,1,0:T(4,128)S(1)}, f32[3,4,512,2048]{3,2,1,0:T(8,128)}) fusion(f32[3,4,512,2048]{3,2,1,0:T(8,128)} %fusion.146, f32[3,4,512]{2,1,0:T(4,128)S(1)} %dynamic-slice_bitcast_fusion.2, pred[512,2048]{1,0:T(8,128)(4,1)S(1)} %iota_compare_fusion.5, bf16[3,2048,4,64]{1,3,2,0:T(8,128)(2,1)} %get-tuple-element.447, ...), kind=kOutput, calls=%fused_computation.18.clone.1 | convolution fusion | flops 1673521152 | bytes 105693184 | tf_op jit(solution)/shard_map/while/body/eval_jaxpr/sbhe,slhe->shbl/dot_general | solution.py:84
  1422.5 41.0 %multiply_convert_fusion.4 = bf16[3,4,512,2048]{3,2,1,0:T(8,128)(2,1)} fusion(f32[3,4,512,2048]{3,2,1,0:T(8,128)} %get-tuple-element.375, f32[3,4,512,2048]{3,2,1,0:T(8,128)} %fusion.146, f32[3,4,512]{2,1,0:T(4,128)S(1)} %get-tuple-element.376, f32[3,4,512]{2,1,0:T(4,128)S(1)} %dynamic-slice_bitcast_fusion.2, pred[512,2048]{1,0:T(8,128)(4,1)S(1)} %iota_compare_fusion.5), kind=kLoop, calls=%fused_computation.17.clone.1 | loop fusion | flops 75497472 | bytes 126926848 | tf_op jit(solution)/shard_map/while/body/eval_jaxpr/convert_element_type | solution.py:88
  1493.6 24.0 bitcast_add_fusion.6
  1518.8 21.6 fusion.146
  1541.8 37.7 %multiply_reduce_fusion.2 = (f32[3,4,512]{2,1,0:T(4,128)S(1)}, f32[3,4,512,2048]{3,2,1,0:T(8,128)}) fusion(f32[3,4,512,2048]{3,2,1,0:T(8,128)} %fusion.146, f32[3,4,512]{2,1,0:T(4,128)S(1)} %dynamic-slice_bitcast_fusion.2, pred[512,2048]{1,0:T(8,128)(4,1)S(1)} %iota_compare_fusion.5, bf16[3,2048,4,64]{1,3,2,0:T(8,128)(2,1)} %get-tuple-element.447, ...), kind=kOutput, calls=%fused_computation.18.clone.1 | convolution fusion | flops 1673521152 | bytes 105693184 | tf_op jit(solution)/shard_map/while/body/eval_jaxpr/sbhe,slhe->shbl/dot_general | solution.py:84
  1579.6 41.2 %multiply_convert_fusion.4 = bf16[3,4,512,2048]{3,2,1,0:T(8,128)(2,1)} fusion(f32[3,4,512,2048]{3,2,1,0:T(8,128)} %get-tuple-element.375, f32[3,4,512,2048]{3,2,1,0:T(8,128)} %fusion.146, f32[3,4,512]{2,1,0:T(4,128)S(1)} %get-tuple-element.376, f32[3,4,512]{2,1,0:T(4,128)S(1)} %dynamic-slice_bitcast_fusion.2, pred[512,2048]{1,0:T(8,128)(4,1)S(1)} %iota_compare_fusion.5), kind=kLoop, calls=%fused_computation.17.clone.1 | loop fusion | flops 75497472 | bytes 126926848 | tf_op jit(solution)/shard_map/while/body/eval_jaxpr/convert_element_type | solution.py:88
  1652.6 25.4 bitcast_add_fusion.6
  1679.2 21.8 fusion.146
  1702.4 37.7 %multiply_reduce_fusion.2 = (f32[3,4,512]{2,1,0:T(4,128)S(1)}, f32[3,4,512,2048]{3,2,1,0:T(8,128)}) fusion(f32[3,4,512,2048]{3,2,1,0:T(8,128)} %fusion.146, f32[3,4,512]{2,1,0:T(4,128)S(1)} %dynamic-slice_bitcast_fusion.2, pred[512,2048]{1,0:T(8,128)(4,1)S(1)} %iota_compare_fusion.5, bf16[3,2048,4,64]{1,3,2,0:T(8,128)(2,1)} %get-tuple-element.447, ...), kind=kOutput, calls=%fused_computation.18.clone.1 | convolution fusion | flops 1673521152 | bytes 105693184 | tf_op jit(solution)/shard_map/while/body/eval_jaxpr/sbhe,slhe->shbl/dot_general | solution.py:84
  1740.1 41.0 %multiply_convert_fusion.4 = bf16[3,4,512,2048]{3,2,1,0:T(8,128)(2,1)} fusion(f32[3,4,512,2048]{3,2,1,0:T(8,128)} %get-tuple-element.375, f32[3,4,512,2048]{3,2,1,0:T(8,128)} %fusion.146, f32[3,4,512]{2,1,0:T(4,128)S(1)} %get-tuple-element.376, f32[3,4,512]{2,1,0:T(4,128)S(1)} %dynamic-slice_bitcast_fusion.2, pred[512,2048]{1,0:T(8,128)(4,1)S(1)} %iota_compare_fusion.5), kind=kLoop, calls=%fused_computation.17.clone.1 | loop fusion | flops 75497472 | bytes 126926848 | tf_op jit(solution)/shard_map/while/body/eval_jaxpr/convert_element_type | solution.py:88
  1812.9 25.4 bitcast_add_fusion.6
  1839.5 21.7 fusion.146
  1862.5 37.7 %multiply_reduce_fusion.2 = (f32[3,4,512]{2,1,0:T(4,128)S(1)}, f32[3,4,512,2048]{3,2,1,0:T(8,128)}) fusion(f32[3,4,512,2048]{3,2,1,0:T(8,128)} %fusion.146, f32[3,4,512]{2,1,0:T(4,128)S(1)} %dynamic-slice_bitcast_fusion.2, pred[512,2048]{1,0:T(8,128)(4,1)S(1)} %iota_compare_fusion.5, bf16[3,2048,4,64]{1,3,2,0:T(8,128)(2,1)} %get-tuple-element.447, ...), kind=kOutput, calls=%fused_computation.18.clone.1 | convolution fusion | flops 1673521152 | bytes 105693184 | tf_op jit(solution)/shard_map/while/body/eval_jaxpr/sbhe,slhe->shbl/dot_general | solution.py:84
  1900.2 41.0 %multiply_convert_fusion.4 = bf16[3,4,512,2048]{3,2,1,0:T(8,128)(2,1)} fusion(f32[3,4,512,2048]{3,2,1,0:T(8,128)} %get-tuple-element.375, f32[3,4,512,2048]{3,2,1,0:T(8,128)} %fusion.146, f32[3,4,512]{2,1,0:T(4,128)S(1)} %get-tuple-element.376, f32[3,4,512]{2,1,0:T(4,128)S(1)} %dynamic-slice_bitcast_fusion.2, pred[512,2048]{1,0:T(8,128)(4,1)S(1)} %iota_compare_fusion.5), kind=kLoop, calls=%fused_computation.17.clone.1 | loop fusion | flops 75497472 | bytes 126926848 | tf_op jit(solution)/shard_map/while/body/eval_jaxpr/convert_element_type | solution.py:88
  1973.0 25.1 bitcast_add_fusion.6
  2025.8 19.2 copy.87
  2054.2 265.0 %all-to-all-done.3 = bf16[3,2048,3,256]{3,0,2,1:T(4,128)(2,1)} async-done(((bf16[3,2048,3,256]{3,0,2,1:T(4,128)(2,1)}), bf16[3,2048,3,256]{3,0,2,1:T(4,128)(2,1)}, u32[]{:S(2)}, u32[]{:S(2)}) %all-to-all-start.3) | async-done | bytes 9437216 | tf_op jit(solution)/shard_map/all_to_all | solution.py:254
  2319.1 25.7 copy.88
  2344.8 25.8 %reshape.281 = bf16[1536,3,16,64]{0,3,2,1:T(8,128)(2,1)} reshape(bf16[3,512,3,4,256]{1,0,4,3,2:T(4,128)(2,1)} %bitcast.204) | data formatting | bytes 18874368 | tf_op jit(solution)/shard_map/reshape | solution.py:255
  2405.4 20.6 fusion.80
  2429.6 19.9 fusion.61
  2449.6 20.0 fusion.74
  2476.6 40.4 %all-reduce.22 = (f32[1024]{0:T(1024)S(1)}, f32[1024]{0:T(1024)S(1)}, f32[3072]{0:T(1024)S(1)}, f32[1024]{0:T(1024)S(1)}, f32[1024]{0:T(1024)S(1)}, /*index=5*/f32[1024]{0:T(1024)S(1)}, f32[4096]{0:T(1024)S(1)}) all-reduce(f32[1024]{0:T(1024)S(1)} %get-tuple-element.170, ...), channel_id=2, replica_groups=mesh['dp'=8,'seq'=4] {'dp','seq'}, use_global_device_ids=true, to_apply=%region_14.15.clone | all-reduce | flops 12288 | bytes 98304
  2531.3 27.4 %reduce-scatter.5.cloned.1.call-done = f32[32,3072]{1,0:T(8,128)} async-done(((f32[1024,3072]{1,0:T(8,128)}), f32[32,3072]{1,0:T(8,128)}) %reduce-scatter.5.cloned.1.call-update) | async-done | bytes 393232 | tf_op jit(solution)/shard_map/reduce_scatter | solution.py:277
  (261 shorter events, 476.3 us)
Async XLA Ops:
  7.2 53.3 %copy-start = (bf16[3,512,1024]{2,1,0:T(8,128)(2,1)S(1)}, bf16[3,512,1024]{2,1,0:T(8,128)(2,1)}, u32[]{:S(2)}) copy-start(bf16[3,512,1024]{2,1,0:T(8,128)(2,1)} %param.18) | copy-start | bytes 9437188
  7.2 6.9 copy-start.36
  7.2 7.1 copy-start.37
  7.2 7.4 copy-start.38
  7.2 7.6 copy-start.39
  7.2 7.8 copy-start.40
  7.2 8.0 copy-start.41
  7.3 8.3 copy-start.42
  7.3 76.0 %all-gather.6.cloned.1.call-start = ((), (), s32[]{:S(2)}) async-start(), calls=%async_computation.8 | async-start | bytes 6488064 | tf_op jit(solution)/shard_map/all_gather | solution.py:129
  8.0 1004.1 %all-gather.10.cloned.1.call-start = ((), (), s32[]{:S(2)}) async-start(), calls=%async_computation.10 | async-start | bytes 8650752 | tf_op jit(solution)/shard_map/all_gather | solution.py:135
  11.1 48.5 %copy-start.20 = (f32[3,512]{1,0:T(4,128)}, f32[3,512]{1,0:T(4,128)S(1)}, u32[]{:S(2)}) copy-start(f32[3,512]{1,0:T(4,128)S(1)} %broadcast_multiply_fusion.1) | copy-start | bytes 18436
  14.0 85.9 %copy-start.16 = (f32[1536]{0:T(1024)}, f32[1536]{0:T(1024)S(1)}, u32[]{:S(2)}) copy-start(f32[1536]{0:T(1024)S(1)} %div.45) | copy-start | bytes 18436
  58.9 41.0 %copy-start.22 = (f32[1024]{0:T(1024)}, f32[1024]{0:T(1024)S(1)}, u32[]{:S(2)}) copy-start(f32[1024]{0:T(1024)S(1)} %convert_element_type.136) | copy-start | bytes 12292
  58.9 41.0 %copy-start.26 = (f32[1024]{0:T(1024)}, f32[1024]{0:T(1024)S(1)}, u32[]{:S(2)}) copy-start(f32[1024]{0:T(1024)S(1)} %convert_element_type.143) | copy-start | bytes 12292
  58.9 41.0 %copy-start.28 = (f32[1024]{0:T(1024)}, f32[1024]{0:T(1024)S(1)}, u32[]{:S(2)}) copy-start(f32[1024]{0:T(1024)S(1)} %convert_element_type.137) | copy-start | bytes 12292
  59.6 40.4 %copy-start.18 = (f32[1536]{0:T(1024)}, f32[1536]{0:T(1024)S(1)}, u32[]{:S(2)}) copy-start(f32[1536]{0:T(1024)S(1)} %rsqrt.16) | copy-start | bytes 18436
  60.4 77.5 %copy-start.12 = (f32[1536,16]{0,1:T(8,128)}, f32[1536,16]{0,1:T(8,128)S(1)}, u32[]{:S(2)}) copy-start(f32[1536,16]{0,1:T(8,128)S(1)} %get-tuple-element.253) | copy-start | bytes 294916
  60.5 77.5 %copy-start.14 = (f32[1536,16]{0,1:T(8,128)}, f32[1536,16]{0,1:T(8,128)S(1)}, u32[]{:S(2)}) copy-start(f32[1536,16]{0,1:T(8,128)S(1)} %get-tuple-element.254) | copy-start | bytes 294916
  144.5 14.1 copy-start.6
  181.2 319.6 %all-to-all-start = ((bf16[3,512,3,1024]{1,0,2,3:T(4,128)(2,1)}), bf16[3,512,3,1024]{1,0,2,3:T(4,128)(2,1)}, u32[]{:S(2)}, u32[]{:S(2)}) async-start(bf16[3,512,3,1024]{1,0,2,3:T(4,128)(2,1)} %copy.75), calls=%async_computation | async-start | bytes 25165824 | tf_op jit(solution)/shard_map/all_to_all | solution.py:183
  187.5 895.4 %all-gather.12.cloned.1.call-start = ((), (), s32[]{:S(2)}) async-start(), calls=%async_computation.11 | async-start | bytes 8650752 | tf_op jit(solution)/shard_map/all_gather | solution.py:137
  839.8 5.6 copy-start.34
  839.8 159.3 %all-to-all-start.1 = ((bf16[3,2048,256]{2,0,1:T(4,128)(2,1)}), bf16[3,2048,256]{2,0,1:T(4,128)(2,1)}, u32[]{:S(2)}, u32[]{:S(2)}) async-start(bf16[3,2048,256]{2,0,1:T(4,128)(2,1)} %reshape.302), calls=%async_computation.1 | async-start | bytes 8388608 | tf_op jit(solution)/shard_map/all_to_all | solution.py:191
  844.8 291.1 %all-gather.8.cloned.1.call-start = ((), (), s32[]{:S(2)}) async-start(), calls=%async_computation.9 | async-start | bytes 2162688 | tf_op jit(solution)/shard_map/all_gather | solution.py:131
  845.4 1685.9 %reduce-scatter.7.cloned.1.call-start = ((), (), s32[]{:S(2)}) async-start(), calls=%async_computation.13 | async-start | bytes 4325376 | tf_op jit(solution)/shard_map/reduce_scatter | solution.py:279
  999.1 7.8 copy-start.4
  1012.0 1519.3 %reduce-scatter.9.cloned.1.call-start = ((), (), s32[]{:S(2)}) async-start(), calls=%async_computation.14 | async-start | bytes 17301504 | tf_op jit(solution)/shard_map/reduce_scatter | solution.py:283
  1012.1 70.8 %copy-start.5 = (bf16[3,512,1024]{2,1,0:T(8,128)(2,1)S(1)}, bf16[3,512,1024]{2,1,0:T(8,128)(2,1)}, u32[]{:S(2)}) copy-start(bf16[3,512,1024]{2,1,0:T(8,128)(2,1)} %param.19) | copy-start | bytes 9437188
  1082.9 33.2 %copy-start.11 = (bf16[1536,1024]{1,0:T(8,128)(2,1)S(1)}, bf16[1536,1024]{1,0:T(8,128)(2,1)}, u32[]{:S(2)}) copy-start(bf16[1536,1024]{1,0:T(8,128)(2,1)} %get-tuple-element.239) | copy-start | bytes 9437188
  1150.1 175.3 %all-to-all-start.2 = ((bf16[3,512,1024]{1,0,2:T(4,128)(2,1)}), bf16[3,512,1024]{1,0,2:T(4,128)(2,1)}, u32[]{:S(2)}, u32[]{:S(2)}) async-start(bf16[3,512,1024]{1,0,2:T(4,128)(2,1)} %copy.84), calls=%async_computation.2 | async-start | bytes 8388608 | tf_op jit(solution)/shard_map/all_to_all | solution.py:217
  1155.1 1376.2 %reduce-scatter.11.cloned.1.call-start = ((), (), s32[]{:S(2)}) async-start(), calls=%async_computation.15 | async-start | bytes 17301504 | tf_op jit(solution)/shard_map/reduce_scatter | solution.py:285
  2045.0 6.7 copy-start.1
  2045.0 6.7 copy-start.21
  2045.0 6.7 copy-start.23
  2045.0 6.7 copy-start.29
  2045.0 6.7 copy-start.30
  2045.0 274.1 %all-to-all-start.3 = ((bf16[3,2048,3,256]{3,0,2,1:T(4,128)(2,1)}), bf16[3,2048,3,256]{3,0,2,1:T(4,128)(2,1)}, u32[]{:S(2)}, u32[]{:S(2)}) async-start(bf16[3,2048,3,256]{3,0,2,1:T(4,128)(2,1)} %copy.87), calls=%async_computation.3 | async-start | bytes 25165824 | tf_op jit(solution)/shard_map/all_to_all | solution.py:254
  2051.6 507.1 %reduce-scatter.5.cloned.1.call-start = ((), (), s32[]{:S(2)}) async-start(), calls=%async_computation.12 | async-start | bytes 12976128 | tf_op jit(solution)/shard_map/reduce_scatter | solution.py:277
  2382.5 4.6 copy-start.10
  2405.4 20.6 copy-start.9
  2405.4 20.6 copy-start.35
  2429.6 20.0 copy-start.17
  2429.6 20.0 copy-start.27
  2449.5 20.1 copy-start.25
  2449.5 20.1 copy-start.2
  2449.6 20.1 copy-start.19
  2469.6 7.0 copy-start.31
  2517.1 41.7 %copy-start.43 = (f32[32]{0:T(128)}, f32[32]{0:T(128)S(1)}, u32[]{:S(2)}) copy-start(f32[32]{0:T(128)S(1)} %dynamic-slice.3) | copy-start | bytes 388
  (8 other events, 10.7 us)
Sparse Core Ops, SparseCore 0:
  10.9 72.2 all-gather.5
  86.2 75.5 all-gather.9
  191.2 268.5 all-gather.11
  848.3 113.5 all-gather.7
  1012.1 148.5 reduce-scatter.6
  1163.4 433.8 reduce-scatter.8
  1600.2 361.9 reduce-scatter.10
  2402.4 156.2 reduce-scatter.4
where the time goes:
time: 2580 us; the launch traced here: 2570 us
  matrix products  888 us (34%)
  waiting for transfers between devices  797 us (31%)
  other arithmetic  344 us (13%)
  local copies, waits for them, and re-layouts  256 us (10%)
  blocking collectives  237 us (9%)
    all_to_all x1, waiting for transfers between devices, local(): lax.all_to_all(sending, 'seq', split_axis=3, concat_axis=1, tiled=True)  313 us
    all_to_all x1, waiting for transfers between devices, local(): lax.all_to_all(grad_stack, 'seq', split_axis=1, concat_axis=3, tiled=True)  265 us
    dot_general x8, matrix products, masked_scores(): jnp.einsum('sbhe,slhe->shbl', query_block, keys, preferred_element_type=j...  174 us
    all_to_all x1, waiting for transfers between devices, local(): lax.all_to_all(grad_context, 'seq', split_axis=2, concat_axis=1, tiled=True)  170 us
    convert_element_type x4, other arithmetic, one_block(): grad_scores = (probability * (grad_prob - inner)).astype(jnp.bfloat16)  164 us
    all_gather x1, blocking collectives, local(): lax.all_gather(expand_bias, ('dp', 'seq'), axis=0, tiled=True)  154 us
    dot_general x4, matrix products, one_block(): jnp.einsum('sbhe,slhe->shbl', grad_block, values, preferred_element_type=...  151 us
    dot_general x4, matrix products, one_block(): jnp.einsum('shbl,sbhe->slhe', rounded, grad_block, preferred_element_type...  99.8 us
  transfers between devices with their start and end apart: 12, of which 5 were waited for; matrix products, arithmetic and copies ran while one was open for 58% of the time, Pallas kernels for 0%

commit v1 on v0

v1 whole, which is shorter than its diff:
```python
import math

import jax
import jax.numpy as jnp
from jax import lax
from jax.experimental import pallas as pl
from jax.experimental.pallas import tpu as pltpu
from jax.sharding import PartitionSpec as P

H = 16
HD = 64
ROT = 16


big_negative = -1e30
epsilon = 1e-05


def layer_norm(values, gain, shift):
    average = jnp.mean(values, axis=-1, keepdims=True)
    centered = values - average
    variance = jnp.mean(centered * centered, axis=-1, keepdims=True)
    return centered * lax.rsqrt(variance + epsilon) * gain + shift


def rotary_tables(positions, width):
    half = ROT // 2
    entry = jnp.arange(HD, dtype=jnp.int32)
    index = (entry % half).astype(jnp.float32)
    frequency = 10000.0 ** (-(index * 2.0 / ROT))
    angles = positions.astype(jnp.float32)[:, None] * frequency[None, :]
    cosine, sine = jnp.cos(angles), jnp.sin(angles)
    keep = jnp.where(entry < ROT, cosine, 1.0)
    ahead = jnp.where(entry < half, -sine, 0.0)
    behind = jnp.where((entry >= half) & (entry < ROT), sine, 0.0)
    return tuple(jnp.tile(table, (1, width // HD)) for table in (keep, ahead, behind))


def shifted(values, amount):
    return jnp.concatenate([values[..., amount:], values[..., :amount]], axis=-1)


def rotate(values, tables, sign):
    keep, ahead, behind = tables
    half = ROT // 2
    return values * keep + sign * (
        shifted(values, half) * ahead + shifted(values, -half) * behind
    )


def attention_body(
    heads,
    block,
    q_ref,
    k_ref,
    v_ref,
    dc_ref,
    kt_ref,
    vt_ref,
    c_ref,
    dq_ref,
    dk_ref,
    dv_ref,
    s_ref,
    dk_acc,
    dv_acc,
):
    qi = pl.program_id(1)
    steps = pl.num_programs(1)
    scale = 1.0 / math.sqrt(HD)
    width = heads * HD

    @pl.when(qi == 0)
    def _():
        dk_acc[...] = jnp.zeros_like(dk_acc)
        dv_acc[...] = jnp.zeros_like(dv_acc)

    lane = lax.broadcasted_iota(jnp.int32, (block, width), 1) // HD
    causal = lax.broadcasted_iota(jnp.int32, (block, block), 0) <= lax.broadcasted_iota(
        jnp.int32, (block, block), 1
    )
    q_all = q_ref[...] * jnp.bfloat16(scale)
    dc_all = dc_ref[...]
    contexts = []
    grads = []
    nt = (((1,), (1,)), ((), ()))
    for h in range(heads):
        zero = jnp.zeros_like(q_all)
        q = jnp.where(lane == h, q_all, zero)
        dc = jnp.where(lane == h, dc_all, zero)
        rows = pl.ds(h * HD, HD)

        def scores(ki, q=q):
            keys = k_ref[pl.ds(ki * block, block), :]
            return lax.dot_general(keys, q, nt, preferred_element_type=jnp.float32)

        def first(ki, highest, scores=scores):
            s = scores(ki)
            s_ref[pl.ds(ki * block, block), :] = s
            return jnp.maximum(highest, jnp.max(s, axis=0, keepdims=True))

        diagonal = jnp.where(causal, scores(qi), big_negative)
        s_ref[pl.ds(qi * block, block), :] = diagonal
        highest = lax.fori_loop(0, qi, first, jnp.max(diagonal, axis=0, keepdims=True))

        def second(ki, carry, highest=highest, rows=rows):
            total, context = carry
            e = jnp.exp(s_ref[pl.ds(ki * block, block), :] - highest)
            total = total + jnp.sum(e, axis=0, keepdims=True)
            context = context + jnp.dot(
                vt_ref[rows, pl.ds(ki * block, block)],
                e.astype(jnp.bfloat16),
                preferred_element_type=jnp.float32,
            )
            return (total, context)

        total, context = lax.fori_loop(
            0,
            qi + 1,
            second,
            (jnp.zeros((1, block), jnp.float32), jnp.zeros((HD, block), jnp.float32)),
        )
        context = context / total
        log_total = highest + jnp.log(total)
        contexts.append(context)
        dct = dc_all[:, h * HD : (h + 1) * HD].astype(jnp.float32).T
        inner = jnp.sum(context * dct, axis=0, keepdims=True)

        def third(ki, grad, q=q, dc=dc, inner=inner, log_total=log_total, rows=rows):
            here = pl.ds(ki * block, block)
            p = jnp.exp(s_ref[here, :] - log_total)
            dp = lax.dot_general(v_ref[here, :], dc, nt, preferred_element_type=jnp.float32)
            ds = (p * (dp - inner)).astype(jnp.bfloat16)
            dv_acc[here, :] += jnp.dot(
                p.astype(jnp.bfloat16), dc, preferred_element_type=jnp.float32
            )
            dk_acc[here, :] += jnp.dot(ds, q, preferred_element_type=jnp.float32)
            return grad + jnp.dot(kt_ref[rows, here], ds, preferred_element_type=jnp.float32)

        grad = lax.fori_loop(0, qi + 1, third, jnp.zeros((HD, block), jnp.float32))
        grads.append(grad * scale)
    c_ref[...] = jnp.concatenate(contexts, axis=0).T.astype(jnp.bfloat16)
    dq_ref[...] = jnp.concatenate(grads, axis=0).T.astype(jnp.bfloat16)

    @pl.when(qi == steps - 1)
    def _():
        dk_ref[...] = dk_acc[...].astype(jnp.bfloat16)
        dv_ref[...] = dv_acc[...].astype(jnp.bfloat16)


def attention(parts):
    _, seqs, length, width = parts.shape
    heads = width // HD
    block = min(512, length)
    turned = parts[1:3].transpose(0, 1, 3, 2)

    def rows_of(which):
        return pl.BlockSpec((None, None, block, width), lambda s, i, w=which: (w, s, i, 0))

    def whole_of(which):
        return pl.BlockSpec((None, None, length, width), lambda s, i, w=which: (w, s, 0, 0))

    def turned_of(which):
        return pl.BlockSpec((None, None, width, length), lambda s, i, w=which: (w, s, 0, 0))

    out_rows = pl.BlockSpec((None, block, width), lambda s, i: (s, i, 0))
    out_whole = pl.BlockSpec((None, length, width), lambda s, i: (s, 0, 0))
    shape = jax.ShapeDtypeStruct((seqs, length, width), jnp.bfloat16)

    def body(*refs):
        attention_body(heads, block, *refs)

    return pl.pallas_call(
        body,
        grid=(seqs, length // block),
        in_specs=[rows_of(0), whole_of(1), whole_of(2), rows_of(3), turned_of(0), turned_of(1)],
        out_specs=[out_rows, out_rows, out_whole, out_whole],
        out_shape=[shape] * 4,
        scratch_shapes=[
            pltpu.VMEM((length, block), jnp.float32),
            pltpu.VMEM((length, width), jnp.float32),
            pltpu.VMEM((length, width), jnp.float32),
        ],
        compiler_params=pltpu.CompilerParams(
            dimension_semantics=("arbitrary", "arbitrary"), vmem_limit_bytes=50 * 1024 * 1024
        ),
        name="attention",
    )(parts, parts, parts, parts, turned, turned)


def scatter_sum(values, axes):
    return lax.psum_scatter(values, axes, scatter_dimension=0, tiled=True)


def local(
    hidden_in,
    cotangent,
    first_gain,
    first_shift,
    triple_weight,
    triple_bias,
    dense_weight,
    dense_bias,
    second_gain,
    second_shift,
    expand_weight,
    expand_bias,
    contract_weight,
    contract_bias,
):
    axes = ("dp", "seq")
    devices = lax.axis_size("dp") * lax.axis_size("seq")
    w_triple = lax.all_gather(triple_weight, axes, axis=0, tiled=True)
    vectors = (
        first_gain,
        first_shift,
        triple_bias,
        dense_bias,
        second_gain,
        second_shift,
        expand_bias,
        contract_bias,
    )
    stacked = lax.all_gather(jnp.concatenate(vectors), axes, axis=0, tiled=True)
    stacked = stacked.reshape(devices, -1)
    whole = []
    offset = 0
    for vector in vectors:
        size = vector.shape[0]
        whole.append(stacked[:, offset : offset + size].reshape(-1))
        offset += size
    gain_one, shift_one, b_triple, b_dense, gain_two, shift_two, b_expand, b_contract = whole
    w_dense = lax.all_gather(dense_weight, axes, axis=0, tiled=True)
    w_expand = lax.all_gather(expand_weight, axes, axis=0, tiled=True)
    w_contract = lax.all_gather(contract_weight, axes, axis=0, tiled=True)
    seqs, part_len, width = hidden_in.shape
    groups = lax.axis_size("seq")
    heads_here = H // groups
    tokens_here = seqs * part_len
    source = hidden_in.astype(jnp.float32).reshape(tokens_here, width)
    normed_one, pull_one = jax.vjp(
        layer_norm, source, gain_one.astype(jnp.float32), shift_one.astype(jnp.float32)
    )
    normed_two, pull_two = jax.vjp(
        layer_norm, source, gain_two.astype(jnp.float32), shift_two.astype(jnp.float32)
    )
    low_one = normed_one.astype(jnp.bfloat16)
    low_two = normed_two.astype(jnp.bfloat16)
    triple = jnp.dot(low_one, w_triple, preferred_element_type=jnp.float32) + b_triple.astype(
        jnp.float32
    )
    positions = lax.axis_index("seq") * part_len + jnp.arange(part_len, dtype=jnp.int32)
    tables = rotary_tables(positions, 2 * width)
    rotated = rotate(triple[:, : 2 * width].reshape(seqs, part_len, 2 * width), tables, 1.0)
    rotated = rotated.astype(jnp.bfloat16).reshape(tokens_here, 2 * width)
    upstream = cotangent.reshape(tokens_here, width)
    grad_context = jnp.einsum("td,ed->te", upstream, w_dense, preferred_element_type=jnp.float32)
    sending = jnp.stack(
        [
            rotated[:, :width],
            rotated[:, width:],
            triple[:, 2 * width :].astype(jnp.bfloat16),
            grad_context.astype(jnp.bfloat16),
        ]
    )
    mine = heads_here * HD
    sending = sending.reshape(4, seqs, part_len, groups, mine).transpose(3, 0, 1, 2, 4)
    received = lax.all_to_all(sending, "seq", split_axis=0, concat_axis=0, tiled=True)
    received = received.transpose(1, 2, 0, 3, 4).reshape(4, seqs, groups * part_len, mine)
    returned = jnp.stack(attention(received))
    returned = returned.reshape(4, seqs, groups, part_len, mine).transpose(2, 0, 1, 3, 4)
    returned = lax.all_to_all(returned, "seq", split_axis=0, concat_axis=0, tiled=True)
    returned = returned.transpose(1, 2, 3, 0, 4).reshape(4, tokens_here, width)
    context_flat = returned[0]
    attended = jnp.dot(context_flat, w_dense, preferred_element_type=jnp.float32) + b_dense.astype(
        jnp.float32
    )
    expanded = jnp.dot(low_two, w_expand, preferred_element_type=jnp.float32) + b_expand.astype(
        jnp.float32
    )
    activated, pull_gelu = jax.vjp(lambda inner: jax.nn.gelu(inner, approximate=False), expanded)
    low_act = activated.astype(jnp.bfloat16)
    contracted = jnp.dot(
        low_act, w_contract, preferred_element_type=jnp.float32
    ) + b_contract.astype(jnp.float32)
    block_out = (source + attended + contracted).astype(jnp.bfloat16).reshape(seqs, part_len, width)
    upstream_total = jnp.sum(upstream.astype(jnp.float32), axis=0)
    grad_w_dense = jnp.einsum(
        "td,te->de", context_flat, upstream, preferred_element_type=jnp.float32
    )
    grad_act = jnp.einsum(
        "td,fd->tf", upstream, w_contract, preferred_element_type=jnp.float32
    )
    grad_expanded = pull_gelu(grad_act)[0].astype(jnp.bfloat16)
    grad_w_contract = jnp.einsum("tf,td->fd", low_act, upstream, preferred_element_type=jnp.float32)
    grad_w_expand = jnp.einsum(
        "td,tf->df", low_two, grad_expanded, preferred_element_type=jnp.float32
    )
    grad_b_expand = jnp.sum(grad_expanded.astype(jnp.float32), axis=0)
    grad_second = jnp.einsum(
        "tf,df->td", grad_expanded, w_expand, preferred_element_type=jnp.float32
    )
    grad_source_two, grad_gain_two, grad_shift_two = pull_two(grad_second)
    grad_pair = jnp.concatenate([returned[1], returned[2]], axis=-1).astype(jnp.float32)
    grad_pair = rotate(grad_pair.reshape(seqs, part_len, 2 * width), tables, -1.0)
    grad_pair = grad_pair.astype(jnp.bfloat16).reshape(tokens_here, 2 * width)
    grad_triple = jnp.concatenate([grad_pair, returned[3]], axis=-1)
    grad_w_triple = jnp.einsum(
        "td,te->de", low_one, grad_triple, preferred_element_type=jnp.float32
    )
    grad_b_triple = jnp.sum(grad_triple.astype(jnp.float32), axis=0)
    grad_first = jnp.einsum(
        "te,de->td", grad_triple, w_triple, preferred_element_type=jnp.float32
    )
    grad_source_one, grad_gain_one, grad_shift_one = pull_one(grad_first)
    grad_input = (upstream.astype(jnp.float32) + grad_source_one + grad_source_two).reshape(
        seqs, part_len, width
    )
    totals = (
        grad_gain_one,
        grad_shift_one,
        grad_b_triple,
        upstream_total,
        grad_gain_two,
        grad_shift_two,
        grad_b_expand,
    )
    totals = [total.reshape(devices, -1) for total in totals]
    sizes = [total.shape[1] for total in totals]
    vector_grads = lax.psum_scatter(
        jnp.concatenate(totals, axis=1), axes, scatter_dimension=0, tiled=True
    ).reshape(-1)
    pieces = []
    offset = 0
    for size in sizes:
        pieces.append(vector_grads[offset : offset + size])
        offset += size
    out_gain_one, out_shift_one, out_b_triple, out_b_dense = pieces[:4]
    out_gain_two, out_shift_two, out_b_expand = pieces[4:]
    out_b_contract = out_b_dense
    out_w_contract = scatter_sum(grad_w_contract, axes)
    out_w_expand = scatter_sum(grad_w_expand, axes)
    out_w_dense = scatter_sum(grad_w_dense, axes)
    out_w_triple = scatter_sum(grad_w_triple, axes)
    return (
        block_out,
        grad_input,
        out_gain_one,
        out_shift_one,
        out_w_triple,
        out_b_triple,
        out_w_dense,
        out_b_dense,
        out_gain_two,
        out_shift_two,
        out_w_expand,
        out_b_expand,
        out_w_contract,
        out_b_contract,
    )


def solution(mesh):
    placed = (
        P("dp", "seq", None),
        P("dp", "seq", None),
        P(("dp", "seq")),
        P(("dp", "seq")),
        P(("dp", "seq"), None),
        P(("dp", "seq")),
        P(("dp", "seq"), None),
        P(("dp", "seq")),
        P(("dp", "seq")),
        P(("dp", "seq")),
        P(("dp", "seq"), None),
        P(("dp", "seq")),
        P(("dp", "seq"), None),
        P(("dp", "seq")),
    )
    return jax.shard_map(
        local,
        mesh=mesh,
        in_specs=placed,
        out_specs=(
            P("dp", "seq", None),
            P("dp", "seq", None),
            P(("dp", "seq")),
            P(("dp", "seq")),
            P(("dp", "seq"), None),
            P(("dp", "seq")),
            P(("dp", "seq"), None),
            P(("dp", "seq")),
            P(("dp", "seq")),
            P(("dp", "seq")),
            P(("dp", "seq"), None),
            P(("dp", "seq")),
            P(("dp", "seq"), None),
            P(("dp", "seq")),
        ),
        check_vma=False,
    )
```

time: 2580 us -> 1900 us (0.74)
  matrix products: 888 us -> 243 us
  blocking collectives: 237 us -> 540 us
  other arithmetic: 344 us -> 90.8 us
  waiting for transfers between devices: 797 us -> 583 us
  Pallas kernels: 0 us -> 176 us
    dot_general x32 -> x4, matrix products: 718 us -> 76.4 us  [the longest x1 32.7 us: local(): jnp.einsum('td,fd->tf', upstream, w_contract, preferred_element_type=jnp....]
    all_to_all x0 -> x1, blocking collectives: none -> 457 us  [local(): lax.all_to_all(returned, 'seq', split_axis=0, concat_axis=0, tiled=True)]
    all_to_all x4 -> x1, waiting for transfers between devices: 748 us -> 438 us  [local(): lax.all_to_all(sending, 'seq', split_axis=0, concat_axis=0, tiled=True)]
    pallas_call x0 -> x1, Pallas kernels: none -> 176 us  [attention(): pl.pallas_call(body, grid=(seqs, length // block), in_specs=[rows_of(0),...]
    all_gather x1 -> x0, blocking collectives: 154 us -> none  [local(): lax.all_gather(expand_bias, ('dp', 'seq'), axis=0, tiled=True)]
    convert_element_type x13 -> x3, other arithmetic: 181 us -> 41.6 us  [the longest x1 19.3 us: local(): grad_pair = grad_pair.astype(jnp.bfloat16).reshape(tokens_here, 2 * width)]
    reduce_sum x4 -> x0, other arithmetic: 87.5 us -> none  [one_block(): total = jnp.sum(weights, axis=-1, keepdims=True)]
    slice x7 -> x19, local copies, waits for them, and re-layouts: 25.8 us -> 106 us  [the longest x4 40.8 us: shifted(): values[..., :amount]]
  transfers between devices with their start and end apart: 12 -> 9, of which waited for: 5 -> 5; matrix products, arithmetic and copies ran while one was open for 58% -> 30% of each run, Pallas kernels for 0% -> 9%
where the time goes in v1:
time: 1900 us
  waiting for transfers between devices  583 us (31%)
  blocking collectives  540 us (28%)
  local copies, waits for them, and re-layouts  244 us (13%)
  matrix products  243 us (13%)
  Pallas kernels  176 us (9%)
  other arithmetic  90.8 us (5%)
    all_to_all x1, blocking collectives, local(): lax.all_to_all(returned, 'seq', split_axis=0, concat_axis=0, tiled=True)  457 us
    all_to_all x1, waiting for transfers between devices, local(): lax.all_to_all(sending, 'seq', split_axis=0, concat_axis=0, tiled=True)  438 us
    pallas_call x1, Pallas kernels, attention(): pl.pallas_call(body, grid=(seqs, length // block), in_specs=[rows_of(0),...  176 us
    unnamed x2, blocking collectives  82.2 us
    reduce_scatter x4, waiting for transfers between devices, scatter_sum(): return lax.psum_scatter(values, axes, scatter_dimension=0, tiled=True)  77.8 us
    dot_general x1, matrix products, local(): jnp.dot(low_two, w_expand, preferred_element_type=jnp.float32)  70.8 us
    another operation x8, local copies, waits for them, and re-layouts, local(): jnp.stack([rotated[:, :width], rotated[:, width:], triple[:, 2 * width:]....  41 us
    slice x4, local copies, waits for them, and re-layouts, shifted(): values[..., :amount]  40.8 us
  transfers between devices with their start and end apart: 9, of which 5 were waited for; matrix products, arithmetic and copies ran while one was open for 30% of the time, Pallas kernels for 9%

profile of v1, /device:TPU:0, one launch (start us, length us, event | category | flops | bytes accessed | tf_op | source)
XLA Modules:
  0.0 1898.6 jit_solution(13261455848725932529)
XLA Ops:
  15.3 5.4 concatenate.58
  21.0 43.3 %all-reduce = bf16[13312]{0:T(1024)(128)(2,1)S(1)} all-reduce(bf16[13312]{0:T(1024)(128)(2,1)S(1)} %dynamic-update-slice), channel_id=1, replica_groups=mesh['dp'=8,'seq'=4] {'dp','seq'}, use_global_device_ids=true, to_apply=%add | all-reduce | flops 13312 | bytes 53248
  69.5 21.3 %all-gather.9.cloned.1.call-done = bf16[1024,4096]{1,0:T(8,128)(2,1)} async-done(((bf16[32,4096]{1,0:T(8,128)(2,1)}), bf16[1024,4096]{1,0:T(8,128)(2,1)}) %all-gather.9.cloned.1.call-update) | async-done | bytes 8388624 | tf_op jit(solution)/shard_map/all_gather | solution.py:234
  90.8 70.8 %multiply_convert_fusion = (bf16[1536,4096]{1,0:T(8,128)(2,1)}, f32[1536,4096]{1,0:T(8,128)}, f32[1536,4096]{1,0:T(8,128)}) fusion(f32[4096]{0:T(1024)S(1)} %fusion.40, bf16[1536,1024]{1,0:T(8,128)(2,1)} %get-tuple-element.48, bf16[1024,4096]{1,0:T(8,128)(2,1)} %all-gather.9.cloned.1.call-done), kind=kOutput, calls=%fused_computation.4 | convolution fusion | flops 13300137984 | bytes 74465280 | tf_op jit(solution)/shard_map/dot_general | solution.py:278
  161.6 8.0 all-gather.11.cloned.1.call-done
  169.6 32.7 %convert_reduce_fusion = (f32[4096]{0:T(1024)}, bf16[1536,4096]{1,0:T(8,128)(2,1)}) fusion(f32[1536,4096]{1,0:T(8,128)} %get-tuple-element.33, bf16[1536,1024]{1,0:T(8,128)(2,1)S(1)} %bitcast.196, bf16[4096,1024]{1,0:T(8,128)(2,1)} %all-gather.11.cloned.1.call-done, f32[1536,4096]{1,0:T(8,128)} %get-tuple-element.68, f32[4096]{0:T(1024)S(1)} %fusion.40), kind=kOutput, calls=%fused_computation.2 | convolution fusion | flops 12991852544 | bytes 74481664 | tf_op jit(solution)/shard_map/td,fd->tf/dot_general | solution.py:291
  202.4 20.2 %fusion.60 = f32[1024,4096]{1,0:T(8,128)} fusion(bf16[1536,1024]{1,0:T(8,128)(2,1)S(1)} %copy-done.19, bf16[1536,4096]{1,0:T(8,128)(2,1)} %get-tuple-element.71), kind=kOutput, calls=%fused_computation.126 | convolution fusion | flops 12884901888 | bytes 32505856 | tf_op jit(solution)/shard_map/td,tf->df/dot_general | solution.py:296
  226.6 5.4 copy.56
  234.6 5.4 copy.57
  242.5 5.4 copy.58
  248.0 6.4 convolution_convert_fusion
  254.4 4.9 stack.33
  263.5 35.0 %all-gather.5.cloned.1.call-done = bf16[1024,3072]{1,0:T(8,128)(2,1)} async-done(((bf16[32,3072]{1,0:T(8,128)(2,1)}), bf16[1024,3072]{1,0:T(8,128)(2,1)}) %all-gather.5.cloned.1.call-update) | async-done | bytes 6291472 | tf_op jit(solution)/shard_map/all_gather | solution.py:213
  298.5 13.0 convolution_add_fusion
  311.5 6.4 copy-done.3
  318.5 11.4 slice.168
  333.8 6.0 copy.61
  342.3 17.4 fusion.55
  359.8 17.6 fusion.7
  377.3 5.3 fusion.56
  386.5 6.0 copy.59
  392.6 6.2 stack.31
  398.8 5.9 copy.60
  404.7 9.5 maximum_bitcast_fusion
  414.2 6.6 all-to-all-start
  420.8 19.5 %fusion.61 = f32[4096,1024]{1,0:T(8,128)} fusion(bf16[1536,4096]{1,0:T(8,128)(2,1)} %get-tuple-element.32, bf16[1536,1024]{1,0:T(8,128)(2,1)S(1)} %bitcast.198), kind=kOutput, calls=%fused_computation.127 | convolution fusion | flops 12884901888 | bytes 32505856 | tf_op jit(solution)/shard_map/tf,td->fd/dot_general | solution.py:295
  440.5 438.3 %all-to-all-done = bf16[4,4,3,512,256]{3,4,2,1,0:T(8,128)(2,1)} async-done(((bf16[4,4,3,512,256]{3,4,2,1,0:T(8,128)(2,1)}), bf16[4,4,3,512,256]{3,4,2,1,0:T(8,128)(2,1)}, u32[]{:S(2)}, u32[]{:S(2)}) %all-to-all-start) | async-done | bytes 12582944 | tf_op jit(solution)/shard_map/all_to_all | solution.py:268
  878.8 16.8 copy.63
  902.8 176.2 %attention.1 = (bf16[3,2048,256]{2,1,0:T(8,128)(2,1)S(1)}, bf16[3,2048,256]{2,1,0:T(8,128)(2,1)}, bf16[3,2048,256]{2,1,0:T(8,128)(2,1)}, bf16[3,2048,256]{2,1,0:T(8,128)(2,1)}) custom-call(bf16[4,3,2048,256]{3,2,1,0:T(8,128)(2,1)} %bitcast.175, bf16[4,3,2048,256]{3,2,1,0:T(8,128)(2,1)} %bitcast.176, bf16[4,3,2048,256]{3,2,1,0:T(8,128)(2,1)} %bitcast.177, ...), custom_call_target="tpu_custom_call" | custom-call | tf_op jit(solution)/shard_map/attention/pallas_call | solution.py:173
  1096.0 5.7 maximum_bitcast_fusion.1
  1101.7 457.3 %all_to_all.10 = bf16[4,4,3,512,256]{3,4,2,1,0:T(8,128)(2,1)S(1)} all-to-all(bf16[4,4,3,512,256]{3,4,2,1,0:T(8,128)(2,1)S(1)} %maximum_bitcast_fusion.1), channel_id=1, replica_groups=mesh['dp'=8,'seq'=4] {'seq'}, dimensions={0} | all-to-all | bytes 25165824 | tf_op jit(solution)/shard_map/all_to_all | solution.py:272
  1564.9 6.2 copy.70
  1575.4 6.9 fusion.59
  1582.3 6.4 copy.77
  1596.6 5.9 copy.72
  1617.1 9.5 fusion.52
  1626.6 12.7 copy.76
  1639.3 13.0 copy.73
  1652.3 19.3 %fusion.9 = bf16[1536,2048]{1,0:T(8,128)(2,1)S(1)} fusion(f32[1536,8]{1,0:T(8,128)} %bitcast.217, f32[1536,2040]{1,0:T(8,128)} %bitcast.191, f32[1536,2040]{1,0:T(8,128)} %bitcast.190, f32[1536,8]{1,0:T(8,128)} %bitcast.216, bf16[1536,1024]{1,0:T(8,128)(2,1)} %bitcast.203, bf16[1536,1024]{1,0:T(8,128)(2,1)S(1)} %bitcast.202, f32[512,2048]{1,0:T(8,128)} %copy.58, ...), kind=kLoop, calls=%fused_computation.29 | loop fusion | flops 40894464 | bytes 50331648 | tf_op jit(solution)/shard_map/convert_element_type | solution.py:306
  1674.4 13.2 fusion.34
  1690.3 19.8 %fusion.58 = f32[1536,1024]{1,0:T(8,128)} fusion(bf16[1536,4096]{1,0:T(8,128)(2,1)} %get-tuple-element.71, bf16[1024,4096]{1,0:T(8,128)(2,1)} %all-gather.9.cloned.1.call-done), kind=kOutput, calls=%fused_computation.124 | convolution fusion | flops 12884901888 | bytes 27262976 | tf_op jit(solution)/shard_map/tf,df->td/dot_general | solution.py:300
  1714.9 17.5 fusion.50
  1732.6 7.7 fusion.27
  1740.5 39.0 %all-reduce.1 = f32[32,384]{1,0:T(8,128)S(1)} all-reduce(f32[32,384]{1,0:T(8,128)S(1)} %concatenate.78), channel_id=2, replica_groups=mesh['dp'=8,'seq'=4] {'dp','seq'}, use_global_device_ids=true, to_apply=%region_13.14.clone | all-reduce | flops 12288 | bytes 98304
  1781.3 6.2 fusion.57
  1787.6 8.9 add_add_fusion.2
  1796.5 16.7 fusion.33
  1813.2 77.8 %reduce-scatter.5.cloned.1.call-done = f32[32,3072]{1,0:T(8,128)} async-done(((f32[1024,3072]{1,0:T(8,128)}), f32[32,3072]{1,0:T(8,128)}) %reduce-scatter.5.cloned.1.call-update) | async-done | bytes 393232 | tf_op jit(solution)/shard_map/reduce_scatter | solution.py:192
  (161 shorter events, 107.7 us)
Async XLA Ops:
  7.2 58.2 %copy-start = (bf16[3,512,1024]{2,1,0:T(8,128)(2,1)S(1)}, bf16[3,512,1024]{2,1,0:T(8,128)(2,1)}, u32[]{:S(2)}) copy-start(bf16[3,512,1024]{2,1,0:T(8,128)(2,1)} %param.14) | copy-start | bytes 9437188
  7.2 83.6 %all-gather.9.cloned.1.call-start = ((), (), s32[]{:S(2)}) async-start(), calls=%async_computation.8 | async-start | bytes 8650752 | tf_op jit(solution)/shard_map/all_gather | solution.py:234
  7.9 161.7 %all-gather.11.cloned.1.call-start = ((), (), s32[]{:S(2)}) async-start(), calls=%async_computation.9 | async-start | bytes 8650752 | tf_op jit(solution)/shard_map/all_gather | solution.py:235
  8.7 239.3 %all-gather.7.cloned.1.call-start = ((), (), s32[]{:S(2)}) async-start(), calls=%async_computation.7 | async-start | bytes 2162688 | tf_op jit(solution)/shard_map/all_gather | solution.py:233
  9.4 289.1 %all-gather.5.cloned.1.call-start = ((), (), s32[]{:S(2)}) async-start(), calls=%async_computation.6 | async-start | bytes 6488064 | tf_op jit(solution)/shard_map/all_gather | solution.py:213
  10.0 1803.2 %reduce-scatter.9.cloned.1.call-start = ((), (), s32[]{:S(2)}) async-start(), calls=%async_computation.12 | async-start | bytes 17301504 | tf_op jit(solution)/shard_map/reduce_scatter | solution.py:192
  12.4 149.1 %copy-start.21 = (f32[1536]{0:T(1024)}, f32[1536]{0:T(1024)S(1)}, u32[]{:S(2)}) copy-start(f32[1536]{0:T(1024)S(1)} %div.38) | copy-start | bytes 18436
  64.4 97.2 %copy-start.20 = (bf16[32,416]{1,0:T(8,128)(2,1)}, bf16[32,416]{1,0:T(8,128)(2,1)S(1)}, u32[]{:S(2)}) copy-start(bf16[32,416]{1,0:T(8,128)(2,1)S(1)} %reshape.416) | copy-start | bytes 79876
  65.1 96.5 %copy-start.25 = (f32[1536]{0:T(1024)}, f32[1536]{0:T(1024)S(1)}, u32[]{:S(2)}) copy-start(f32[1536]{0:T(1024)S(1)} %add.123) | copy-start | bytes 18436
  65.1 96.5 %copy-start.23 = (f32[1536]{0:T(1024)}, f32[1536]{0:T(1024)S(1)}, u32[]{:S(2)}) copy-start(f32[1536]{0:T(1024)S(1)} %rsqrt.13) | copy-start | bytes 18436
  65.2 96.4 %copy-start.29 = (f32[1024]{0:T(1024)}, f32[1024]{0:T(1024)S(1)}, u32[]{:S(2)}) copy-start(f32[1024]{0:T(1024)S(1)} %reshape.433) | copy-start | bytes 12292
  65.3 96.4 %copy-start.31 = (f32[1024]{0:T(1024)}, f32[1024]{0:T(1024)S(1)}, u32[]{:S(2)}) copy-start(f32[1024]{0:T(1024)S(1)} %reshape.429) | copy-start | bytes 12292
  90.8 78.9 %copy-start.7 = (bf16[3,512,1024]{2,1,0:T(8,128)(2,1)S(1)}, bf16[3,512,1024]{2,1,0:T(8,128)(2,1)}, u32[]{:S(2)}) copy-start(bf16[3,512,1024]{2,1,0:T(8,128)(2,1)} %param.15) | copy-start | bytes 9437188
  169.6 32.7 %copy-start.19 = (bf16[1536,1024]{1,0:T(8,128)(2,1)S(1)}, bf16[1536,1024]{1,0:T(8,128)(2,1)}, u32[]{:S(2)}) copy-start(bf16[1536,1024]{1,0:T(8,128)(2,1)} %get-tuple-element.48) | copy-start | bytes 9437188
  311.5 6.5 copy-start.3
  342.3 17.4 copy-start.4
  386.5 18.1 copy-start.13
  414.2 6.7 copy-start.8
  414.2 464.6 %all-to-all-start = ((bf16[4,4,3,512,256]{3,4,2,1,0:T(8,128)(2,1)}), bf16[4,4,3,512,256]{3,4,2,1,0:T(8,128)(2,1)}, u32[]{:S(2)}, u32[]{:S(2)}) async-start(bf16[4,4,3,512,256]{3,4,2,1,0:T(8,128)(2,1)} %maximum_bitcast_fusion), calls=%async_computation | async-start | bytes 25165824 | tf_op jit(solution)/shard_map/all_to_all | solution.py:268
  420.8 1392.4 %reduce-scatter.11.cloned.1.call-start = ((), (), s32[]{:S(2)}) async-start(), calls=%async_computation.13 | async-start | bytes 17301504 | tf_op jit(solution)/shard_map/reduce_scatter | solution.py:192
  440.4 1372.8 %reduce-scatter.7.cloned.1.call-start = ((), (), s32[]{:S(2)}) async-start(), calls=%async_computation.11 | async-start | bytes 4325376 | tf_op jit(solution)/shard_map/reduce_scatter | solution.py:192
  1081.9 14.1 copy-start.15
  1564.9 37.7 %copy-start.2 = (bf16[1,3,512,4,256]{2,4,3,1,0:T(8,128)(2,1)}, bf16[1,3,512,4,256]{2,4,3,1,0:T(8,128)(2,1)S(1)}, u32[]{:S(2)}) copy-start(bf16[1,3,512,4,256]{2,4,3,1,0:T(8,128)(2,1)S(1)} %get-tuple-element.36) | copy-start | bytes 9437188
  1573.7 1.7 copy-start.17
  1582.3 308.7 %reduce-scatter.5.cloned.1.call-start = ((), (), s32[]{:S(2)}) async-start(), calls=%async_computation.10 | async-start | bytes 12976128 | tf_op jit(solution)/shard_map/reduce_scatter | solution.py:192
  1603.3 6.7 copy-start.16
  1639.3 13.0 copy-start.14
  1652.3 22.1 %copy-start.11 = (bf16[192,8,4,256]{3,1,2,0:T(8,128)(2,1)S(1)}, bf16[192,8,4,256]{3,1,2,0:T(8,128)(2,1)}, u32[]{:S(2)}) copy-start(bf16[192,8,4,256]{3,1,2,0:T(8,128)(2,1)} %copy.82) | copy-start | bytes 9437188
  1652.3 22.1 %copy-start.18 = (bf16[1536,1024]{1,0:T(8,128)(2,1)S(1)}, bf16[1536,1024]{1,0:T(8,128)(2,1)}, u32[]{:S(2)}) copy-start(bf16[1536,1024]{1,0:T(8,128)(2,1)} %get-tuple-element.49) | copy-start | bytes 9437188
  1671.7 2.8 copy-start.5
  1687.6 1.9 copy-start.9
  1687.6 2.6 copy-start.28
  1687.6 2.6 copy-start.27
  1690.3 19.8 %copy-start.12 = (bf16[192,8,4,256]{3,1,2,0:T(8,128)(2,1)S(1)}, bf16[192,8,4,256]{3,1,2,0:T(8,128)(2,1)}, u32[]{:S(2)}) copy-start(bf16[192,8,4,256]{3,1,2,0:T(8,128)(2,1)} %copy.82) | copy-start | bytes 9437188
  1710.1 4.8 copy-start.1
  1710.1 4.8 copy-start.22
  1710.1 4.8 copy-start.30
  1710.1 4.8 copy-start.32
  1714.9 17.7 copy-start.26
  1714.9 17.7 copy-start.24
  1732.5 8.0 copy-start.33
  1780.1 110.9 %copy-start.34 = (f32[32]{0:T(128)}, f32[32]{0:T(128)S(1)}, u32[]{:S(2)}) copy-start(f32[32]{0:T(128)S(1)} %get-tuple-element.101) | copy-start | bytes 388
  1781.3 6.2 copy-start.6
  1781.3 6.2 copy-start.10
  1781.3 15.2 slice-start
  1787.6 8.9 slice-start.1
Sparse Core Ops, SparseCore 0:
  10.9 79.7 all-gather.8
  93.7 75.9 all-gather.10
  172.6 54.9 all-gather.6
  230.3 68.0 all-gather.4
  301.2 626.7 reduce-scatter.8
  930.7 577.0 reduce-scatter.10
  1582.4 147.7 reduce-scatter.6
  1736.8 154.1 reduce-scatter.4
